TPU v7x, 32 devices: a whole 2x2x4 slice. The times are simulated.
32 devices in a mesh: context: 2 (over core), fheads: 4 (over y, x), seqs: 4 (over z).
Axes of the slice: x: 2, y: 2, z: 4, core: 2. Of those that a mesh axis runs over, the one named last changes fastest.
Arguments:
- query_rows: bfloat16 [4096, 3072], P(('seqs', 'context'), 'fheads'), parts along dimension 0, may hold values from -5 to 5
- key_rows: bfloat16 [4096, 3072], P(('seqs', 'context'), 'fheads'), parts along dimension 0, may hold values from -5 to 5
- value_rows: bfloat16 [4096, 3072], P(('seqs', 'context'), 'fheads'), parts along dimension 0, may hold values from -10 to 10
- step_sizes: float32 [4096, 4], P(('seqs', 'context'), 'fheads'), parts along dimension 0, may hold values from 2e-05 to 0.0018
- w_gate: bfloat16 [4, 768, 768], P('fheads', 'context'), may hold values from -4 to 4
- w_up: bfloat16 [4, 768, 768], P('fheads', 'context'), may hold values from -4 to 4
- w_down: bfloat16 [4, 768, 768], P('fheads', 'context'), may hold values from -4 to 4
Outputs:
- window_out: bfloat16 [4096, 3072], P(('seqs', 'context'), 'fheads'), parts along dimension 0
- fast_out: bfloat16 [4096, 3072], P(('seqs', 'context'), 'fheads'), parts along dimension 0
There are 4 independent parts, one for each index of `seqs`. A program takes and returns all parts, laid end to end along the dimension named above; an argument that names none is the same for every part. Nothing has to cross between parts.
All inputs are finite; a program needn't handle non-finite values.
Results may differ from a plain program's by a relative error of at most 0.035.
Values may be sent and summed in bfloat16 or wider, within the bound.
No kernel may reach another device: no remote copies, remote signals or barrier semaphores. Data moves between devices by JAX's collectives and lax.ppermute only.
A program may use at most 128 MiB of HBM per device.

v0:
```python
import math

import jax
import jax.numpy as jnp
from jax import lax
from jax.sharding import PartitionSpec as P

HD = 128
WINDOW = 512


def passed_along(x, axis, by):
    peers = lax.axis_size(axis)
    pairs = [(i, i + by) for i in range(peers) if 0 <= i + by < peers]
    return lax.ppermute(x, axis, pairs)


def unit_rows(values):
    return values * lax.rsqrt(jnp.mean(values * values, axis=-1, keepdims=True) + 1e-06)


def window_block(queries, keys_near, values_near, first_pos):
    row_count = queries.shape[0]
    query_pos = first_pos + jnp.arange(row_count, dtype=jnp.int32)
    key_pos = first_pos - WINDOW + jnp.arange(row_count + WINDOW, dtype=jnp.int32)
    allowed = (
        (key_pos[None, :] >= 0)
        & (key_pos[None, :] <= query_pos[:, None])
        & (key_pos[None, :] > query_pos[:, None] - WINDOW)
    )
    scores = jnp.einsum(
        "ihd,jhd->hij", queries, keys_near, preferred_element_type=jnp.float32
    ) / math.sqrt(HD)
    scores = jnp.where(allowed[None], scores, -1e30)
    row_max = jnp.max(scores, axis=-1, keepdims=True)
    powers = jnp.exp(scores - row_max)
    weights = (powers / jnp.sum(powers, axis=-1, keepdims=True)).astype(jnp.bfloat16)
    attended = jnp.einsum("hij,jhd->ihd", weights, values_near, preferred_element_type=jnp.float32)
    return attended.astype(jnp.bfloat16)


def dot_rows(first_op, second_op):
    return lax.dot_general(
        first_op, second_op, (((0,), (0,)), ((), ())), preferred_element_type=jnp.float32
    )


def dot_back(first_op, second_op):
    return lax.dot_general(
        first_op, second_op, (((1,), (1,)), ((), ())), preferred_element_type=jnp.float32
    )


def renormed(weight, gradient):
    initial = weight.astype(jnp.float32)
    fresh_rows = initial - gradient
    old_ms = jnp.mean(initial * initial, axis=0)
    new_ms = jnp.mean(fresh_rows * fresh_rows, axis=0)
    return (fresh_rows * jnp.sqrt(old_ms) * lax.rsqrt(new_ms + 1e-06)).astype(jnp.bfloat16)


def apply_fast(fast_queries, gate_w, up_w, down_w):
    gate_new = jnp.dot(fast_queries, gate_w, preferred_element_type=jnp.float32)
    up_new = jnp.dot(fast_queries, up_w, preferred_element_type=jnp.float32)
    hidden_new = (gate_new * jax.nn.sigmoid(gate_new) * up_new).astype(jnp.bfloat16)
    return jnp.dot(hidden_new, down_w, preferred_element_type=jnp.float32).astype(jnp.bfloat16)


def body(query_rows, key_rows, value_rows, step_sizes, w_gate, w_up, w_down):
    row_count = query_rows.shape[0]
    heads_here = query_rows.shape[1] // HD
    rim_keys, rim_values = passed_along((key_rows, value_rows), "context", 1)
    first_pos = lax.axis_index("context") * row_count
    keys_near = jnp.concatenate([rim_keys, key_rows], axis=0).reshape(
        row_count + WINDOW, heads_here, HD
    )
    values_near = jnp.concatenate([rim_values, value_rows], axis=0).reshape(
        row_count + WINDOW, heads_here, HD
    )
    window_out = window_block(
        query_rows.reshape(row_count, heads_here, HD), keys_near, values_near, first_pos
    )
    window_out = window_out.reshape(row_count, heads_here * HD)
    gathered = (
        lax.all_gather(w_gate, "context", axis=1, tiled=True),
        lax.all_gather(w_up, "context", axis=1, tiled=True),
        lax.all_gather(w_down, "context", axis=1, tiled=True),
    )
    gate_w = gathered[0][0]
    up_w = gathered[1][0]
    down_w = gathered[2][0]
    fast_keys = unit_rows(key_rows.astype(jnp.float32)).astype(jnp.bfloat16)
    fast_queries = unit_rows(query_rows.astype(jnp.float32)).astype(jnp.bfloat16)
    target = (-(step_sizes * value_rows.astype(jnp.float32))).astype(jnp.bfloat16)
    gate_pre = jnp.dot(fast_keys, gate_w, preferred_element_type=jnp.float32)
    up_pre = jnp.dot(fast_keys, up_w, preferred_element_type=jnp.float32)
    sigmoid_gate = jax.nn.sigmoid(gate_pre)
    hidden = (gate_pre * sigmoid_gate * up_pre).astype(jnp.bfloat16)
    back_grad = dot_back(target, down_w)
    d_gate = (back_grad * up_pre * sigmoid_gate * (1.0 + gate_pre * (1.0 - sigmoid_gate))).astype(
        jnp.bfloat16
    )
    d_up = (back_grad * gate_pre * sigmoid_gate).astype(jnp.bfloat16)
    grad_gate = dot_rows(fast_keys, d_gate)
    grad_up = dot_rows(fast_keys, d_up)
    grad_down = dot_rows(hidden, target)
    summed = (
        lax.psum(grad_gate.astype(jnp.bfloat16), "context").astype(jnp.float32),
        lax.psum(grad_up.astype(jnp.bfloat16), "context").astype(jnp.float32),
        lax.psum(grad_down.astype(jnp.bfloat16), "context").astype(jnp.float32),
    )
    updated_gate = renormed(gate_w, summed[0])
    updated_up = renormed(up_w, summed[1])
    updated_down = renormed(down_w, summed[2])
    fast_out = apply_fast(fast_queries, updated_gate, updated_up, updated_down)
    return (window_out, fast_out)


def solution(mesh):
    in_specs = (
        P(("seqs", "context"), "fheads"),
        P(("seqs", "context"), "fheads"),
        P(("seqs", "context"), "fheads"),
        P(("seqs", "context"), "fheads"),
        P("fheads", "context", None),
        P("fheads", "context", None),
        P("fheads", "context", None),
    )
    out_specs = (P(("seqs", "context"), "fheads"), P(("seqs", "context"), "fheads"))
    return jax.shard_map(body, mesh=mesh, in_specs=in_specs, out_specs=out_specs, check_vma=False)
```

profile of v0, /device:TPU:3, one launch (start us, length us, event | category | flops | bytes accessed | tf_op | source)
XLA Modules:
  0.0 100.2 jit_solution(16830201598666049020)
XLA Ops:
  7.2 0.0 copy-start
  7.2 0.0 copy-start.7
  7.2 0.0 all-gather.4.cloned.1.call-start
  7.2 0.7 all-gather.4.cloned.1.call-update
  7.9 0.0 all-gather.8.cloned.1.call-start
  8.0 0.7 all-gather.8.cloned.1.call-update
  8.7 0.0 all-gather.6.cloned.1.call-start
  8.7 0.0 copy-done
  8.7 0.3 copy.14
  9.0 1.3 %collective-permute-start.1 = (bf16[512,768]{0,1:T(8,128)(2,1)S(1)}, bf16[512,768]{0,1:T(8,128)(2,1)}, u32[]{:S(2)}, u32[]{:S(2)}) collective-permute-start(bf16[512,768]{0,1:T(8,128)(2,1)S(1)} %copy.14), channel_id=1, source_target_pairs={{0,16},{1,17},{2,18},{3,19},{4,20},{5,21},{6,22},{7,23},{8,24},{9,... | collective-permute-start | bytes 2359304 | tf_op jit(solution)/shard_map/ppermute | solution.py:15
  10.3 0.0 copy-done.7
  10.3 1.3 %collective-permute-start = (bf16[512,768]{1,0:T(8,128)(2,1)S(1)}, bf16[512,768]{1,0:T(8,128)(2,1)}, u32[]{:S(2)}, u32[]{:S(2)}) collective-permute-start(bf16[512,768]{1,0:T(8,128)(2,1)S(1)} %copy-done.7), channel_id=1, source_target_pairs={{0,16},{1,17},{2,18},{3,19},{4,20},{5,21},{6,22},{7,23},{8,24},{9,... | collective-permute-start | bytes 2359304 | tf_op jit(solution)/shard_map/ppermute | solution.py:15
  11.6 0.0 all-gather.6.cloned.1.call-update
  11.6 0.0 all-reduce.3.cloned.1.call-start
  11.7 0.2 fusion.11
  11.9 8.8 %all-gather.4.cloned.1.call-done = bf16[1,768,768]{2,1,0:T(8,128)(2,1)} async-done(((bf16[1,384,768]{2,1,0:T(8,128)(2,1)}), bf16[1,768,768]{2,1,0:T(8,128)(2,1)}) %all-gather.4.cloned.1.call-update) | async-done | bytes 1179664 | tf_op jit(solution)/shard_map/all_gather | solution.py:85
  20.7 3.3 %fusion.21 = f32[512,768]{1,0:T(8,128)} fusion(bf16[1,768,768]{2,1,0:T(8,128)(2,1)} %all-gather.4.cloned.1.call-done, bf16[512,768]{1,0:T(8,128)(2,1)S(1)} %copy-done, f32[512]{0:T(512)S(1)} %add_rsqrt_fusion.3), kind=kOutput, calls=%fused_computation.53 | convolution fusion | flops 605159424 | bytes 3540992 | tf_op jit(solution)/shard_map/dot_general | solution.py:95
  24.0 0.0 copy-start.8
  24.0 8.7 %all-gather.8.cloned.1.call-done = bf16[1,768,768]{2,1,0:T(8,128)(2,1)} async-done(((bf16[1,384,768]{2,1,0:T(8,128)(2,1)}), bf16[1,768,768]{2,1,0:T(8,128)(2,1)}) %all-gather.8.cloned.1.call-update) | async-done | bytes 1179664 | tf_op jit(solution)/shard_map/all_gather | solution.py:86
  32.7 0.0 copy-start.9
  32.7 2.2 %fusion.16 = f32[512,768]{1,0:T(8,128)S(1)} fusion(bf16[1,768,768]{2,1,0:T(8,128)(2,1)} %all-gather.8.cloned.1.call-done, bf16[512,768]{1,0:T(8,128)(2,1)S(1)} %copy-done, f32[512]{0:T(512)S(1)} %add_rsqrt_fusion.3), kind=kOutput, calls=%fused_computation.48 | convolution fusion | flops 605159424 | bytes 3540992 | tf_op jit(solution)/shard_map/dot_general | solution.py:96
  34.9 0.0 copy-start.11
  34.9 1.1 %copy-done.11 = f32[512,768]{1,0:T(8,128)} copy-done((f32[512,768]{1,0:T(8,128)}, f32[512,768]{1,0:T(8,128)S(1)}, u32[]{:S(2)}) %copy-start.11) | copy-done | bytes 1572888
  36.1 0.0 copy-done.8
  36.1 0.0 copy-done.9
  36.1 2.1 %convolution_convert_fusion = bf16[768,768]{1,0:T(8,128)(2,1)} fusion(f32[512,768]{1,0:T(8,128)S(1)} %fusion.16, f32[512,768]{1,0:T(8,128)S(1)} %copy-done.9, bf16[512,768]{1,0:T(8,128)(2,1)S(1)} %copy-done.7, f32[512]{0:T(512)S(1)} %bitcast.56), kind=kOutput, calls=%fused_computation.41 | convolution fusion | flops 608501760 | bytes 5113856 | tf_op jit(solution)/shard_map/dot_general | solution.py:43
  38.2 6.5 %all-gather.6.cloned.1.call-done = bf16[1,768,768]{2,1,0:T(8,128)(2,1)} async-done(((bf16[1,384,768]{2,1,0:T(8,128)(2,1)}), bf16[1,768,768]{2,1,0:T(8,128)(2,1)}) %all-gather.6.cloned.1.call-update) | async-done | bytes 1179664 | tf_op jit(solution)/shard_map/all_gather | solution.py:87
  44.7 0.0 copy-start.10
  44.7 0.0 copy-start.12
  44.7 2.2 %fusion.19 = f32[512,768]{1,0:T(8,128)S(1)} fusion(bf16[1,768,768]{2,1,0:T(8,128)(2,1)} %all-gather.6.cloned.1.call-done, bf16[512,768]{1,0:T(8,128)(2,1)S(1)} %copy-done.7, f32[512]{0:T(512)S(1)} %bitcast.57), kind=kOutput, calls=%fused_computation.51 | convolution fusion | flops 605552640 | bytes 3540992 | tf_op jit(solution)/shard_map/dot_general | solution.py:49
  46.9 0.0 copy-done.10
  47.0 0.0 copy-done.12
  47.0 2.2 %convolution_convert_fusion.2 = bf16[768,768]{1,0:T(8,128)(2,1)} fusion(f32[512,768]{1,0:T(8,128)S(1)} %copy-done.10, f32[512,768]{1,0:T(8,128)S(1)} %fusion.19, f32[512,768]{1,0:T(8,128)S(1)} %copy-done.12, bf16[512,768]{1,0:T(8,128)(2,1)S(1)} %copy-done, f32[512]{0:T(512)S(1)} %add_rsqrt_fusion.3), kind=kOutput, calls=%fused_computation.43 | convolution fusion | flops 609681408 | bytes 6686720 | tf_op jit(solution)/shard_map/dot_general | solution.py:43
  49.2 2.1 %convolution_convert_fusion.1 = bf16[768,768]{1,0:T(8,128)(2,1)} fusion(f32[512,768]{1,0:T(8,128)S(1)} %fusion.19, f32[512,768]{1,0:T(8,128)S(1)} %copy-done.10, bf16[512,768]{1,0:T(8,128)(2,1)S(1)} %copy-done, f32[512]{0:T(512)S(1)} %add_rsqrt_fusion.3), kind=kOutput, calls=%fused_computation.42 | convolution fusion | flops 608108544 | bytes 5113856 | tf_op jit(solution)/shard_map/dot_general | solution.py:43
  51.3 0.0 copy-start.1
  51.3 0.0 all-reduce.3.cloned.1.call-update
  51.4 1.1 %copy-done.1 = bf16[512,768]{1,0:T(8,128)(2,1)S(1)} copy-done((bf16[512,768]{1,0:T(8,128)(2,1)S(1)}, bf16[512,768]{1,0:T(8,128)(2,1)}, u32[]{:S(2)}) %copy-start.1) | copy-done | bytes 786456
  52.4 1.2 %copy.16 = bf16[512,768]{0,1:T(8,128)(2,1)} copy(bf16[512,768]{1,0:T(8,128)(2,1)S(1)} %copy-done.1) | data formatting | bytes 1572864 | tf_op args[0]
  53.6 0.2 fusion.9
  53.8 1.8 %compare_and_fusion = pred[512,1024]{0,1:T(8,128)(4,1)} fusion(s32[512]{0:T(512)S(1)} %get-tuple-element.18, s32[512]{0:T(512)S(1)} %get-tuple-element.17, s32[1024]{0:T(1024)S(1)} %iota_add_fusion, pred[1024]{0:T(1024)(128)(4,1)S(1)} %broadcast_compare_fusion), kind=kLoop, calls=%fused_computation.24 | loop fusion | flops 2097152 | bytes 533504 | tf_op jit(solution)/shard_map/and | solution.py:27
  55.6 0.0 collective-permute-done
  55.6 1.5 %pad_maximum_fusion = bf16[1024,768]{1,0:T(8,128)(2,1)S(1)} fusion(bf16[512,768]{1,0:T(8,128)(2,1)} %param.9, bf16[512,768]{1,0:T(8,128)(2,1)} %collective-permute-done), kind=kLoop, calls=%fused_computation.33 | loop fusion | flops 3145728 | bytes 3145728 | tf_op jit(solution)/shard_map/concatenate | solution.py:77
  57.1 1.7 %copy.13 = bf16[1024,768]{0,1:T(8,128)(2,1)} copy(bf16[1024,768]{1,0:T(8,128)(2,1)S(1)} %pad_maximum_fusion) | data formatting | bytes 3145728 | tf_op jit(solution)/shard_map/concatenate | solution.py:77
  58.7 0.0 collective-permute-done.1
  58.7 2.8 %pad_maximum_fusion.1 = bf16[1024,768]{0,1:T(8,128)(2,1)} fusion(bf16[512,768]{0,1:T(8,128)(2,1)S(1)} %copy.14, bf16[512,768]{0,1:T(8,128)(2,1)} %collective-permute-done.1), kind=kLoop, calls=%fused_computation.34 | loop fusion | flops 3145728 | bytes 3145728 | tf_op jit(solution)/shard_map/concatenate | solution.py:74
  61.5 0.0 copy-start.2
  61.5 12.6 %fusion.45 = (f32[6,512]{1,0:T(8,128)S(1)}, f32[6,512,1024]{1,2,0:T(8,128)}) fusion(pred[512,1024]{0,1:T(8,128)(4,1)} %compare_and_fusion, bf16[1024,6,128]{0,2,1:T(8,128)(2,1)} %bitcast.53, bf16[512,6,128]{0,2,1:T(8,128)(2,1)} %bitcast.54), kind=kOutput, calls=%fused_computation.81 | convolution fusion | flops 817890304 | bytes 15478784 | tf_op jit(solution)/shard_map/sub | solution.py:36
  74.1 0.0 copy-done.2
  74.1 6.0 %fusion.13 = bf16[6,128,512]{2,1,0:T(8,128)(2,1)S(1)} fusion(bf16[1024,6,128]{0,2,1:T(8,128)(2,1)S(1)} %bitcast.52, f32[6,512,1024]{1,2,0:T(8,128)} %get-tuple-element.16, f32[6,512]{1,0:T(8,128)S(1)} %get-tuple-element.15), kind=kOutput, calls=%fused_computation.45 | convolution fusion | flops 811991040 | bytes 14954496 | tf_op jit(solution)/shard_map/hij,jhd->ihd/dot_general | solution.py:38
  80.1 1.2 %copy.20 = bf16[512,768]{1,0:T(8,128)(2,1)} copy(bf16[512,768]{0,1:T(8,128)(2,1)S(1)} %bitcast.55) | data formatting | bytes 1572864
  81.3 0.0 all-reduce.3.cloned.1.call-done
  81.3 0.0 copy-start.3
  81.3 0.0 copy-start.4
  81.3 3.6 %fusion.6 = (f32[768]{0:T(1024)S(1)}, f32[768]{0:T(1024)S(1)}, f32[768]{0:T(1024)S(1)}, f32[768]{0:T(1024)S(1)}) fusion(bf16[1,768,768]{2,1,0:T(8,128)(2,1)} %all-gather.4.cloned.1.call-done, bf16[768,768]{1,0:T(8,128)(2,1)} %get-tuple-element.13, bf16[768,768]{1,0:T(8,128)(2,1)} %get-tuple-element.14, bf16[1,768,768]{2,1,0:T(8,128)(2,1)} %all-gather.8.cloned.1.call-done), kind=kLoop, calls=%fused_computation.15 | loop fusion | flops 8254464 | bytes 4730880 | tf_op jit(solution)/shard_map/reduce_sum | solution.py:57
  84.9 0.0 copy-start.5
  84.9 0.0 copy-start.6
  84.9 0.0 copy-done.3
  84.9 0.0 copy-done.4
  85.0 0.6 fusion.8
  85.5 0.6 copy-done.5
  86.1 0.4 copy-done.6
  86.5 2.1 %fusion.14 = f32[512,768]{1,0:T(8,128)} fusion(bf16[768,768]{1,0:T(8,128)(2,1)S(1)} %copy-done.6, bf16[1,768,768]{2,1,0:T(8,128)(2,1)S(1)} %copy-done.5, f32[768]{0:T(1024)S(1)} %add_rsqrt_fusion.2, f32[768]{0:T(1024)S(1)} %multiply_sqrt_fusion.2, bf16[512,768]{1,0:T(8,128)(2,1)S(1)} %copy-done.1, f32[512]{0:T(512)S(1)} %add_rsqrt_fusion.4), kind=kOutput, calls=%fused_computation.46 | convolution fusion | flops 608698368 | bytes 4726784 | tf_op jit(solution)/shard_map/dot_general | solution.py:63
  88.6 5.1 %convolution_convert_fusion.3 = bf16[512,768]{1,0:T(8,128)(2,1)} fusion(bf16[768,768]{1,0:T(8,128)(2,1)} %get-tuple-element.12, bf16[1,768,768]{2,1,0:T(8,128)(2,1)S(1)} %copy-done.3, f32[768]{0:T(1024)S(1)} %get-tuple-element.21, f32[768]{0:T(1024)S(1)} %get-tuple-element.22, f32[512,768]{1,0:T(8,128)} %fusion.14, bf16[768,768]{1,0:T(8,128)(2,1)} %get-tuple-element.14, ...), kind=kOutput, calls=%fused_computation.44 | convolution fusion | flops 1218969600 | bytes 7878656 | tf_op jit(solution)/shard_map/dot_general | solution.py:66
  (10 shorter events, 0.1 us)
Async XLA Ops:
  7.2 1.6 %copy-start = (bf16[512,768]{1,0:T(8,128)(2,1)S(1)}, bf16[512,768]{1,0:T(8,128)(2,1)}, u32[]{:S(2)}) copy-start(bf16[512,768]{1,0:T(8,128)(2,1)} %param.8) | copy-start | bytes 2359300
  7.2 3.1 %copy-start.7 = (bf16[512,768]{1,0:T(8,128)(2,1)S(1)}, bf16[512,768]{1,0:T(8,128)(2,1)}, u32[]{:S(2)}) copy-start(bf16[512,768]{1,0:T(8,128)(2,1)} %param.9) | copy-start | bytes 2359300
  7.2 13.6 %all-gather.4.cloned.1.call-start = ((), (), s32[]{:S(2)}) async-start(), calls=%async_computation | async-start | bytes 1769472 | tf_op jit(solution)/shard_map/all_gather | solution.py:85
  7.9 24.8 %all-gather.8.cloned.1.call-start = ((), (), s32[]{:S(2)}) async-start(), calls=%async_computation.2 | async-start | bytes 1769472 | tf_op jit(solution)/shard_map/all_gather | solution.py:86
  8.7 36.0 %all-gather.6.cloned.1.call-start = ((), (), s32[]{:S(2)}) async-start(), calls=%async_computation.1 | async-start | bytes 1769472 | tf_op jit(solution)/shard_map/all_gather | solution.py:87
  9.0 49.7 %collective-permute-start.1 = (bf16[512,768]{0,1:T(8,128)(2,1)S(1)}, bf16[512,768]{0,1:T(8,128)(2,1)}, u32[]{:S(2)}, u32[]{:S(2)}) collective-permute-start(bf16[512,768]{0,1:T(8,128)(2,1)S(1)} %copy.14), channel_id=1, source_target_pairs={{0,16},{1,17},{2,18},{3,19},{4,20},{5,21},{6,22},{7,23},{8,24},{9,... | collective-permute-start | bytes 2359304 | tf_op jit(solution)/shard_map/ppermute | solution.py:15
  10.3 45.3 %collective-permute-start = (bf16[512,768]{1,0:T(8,128)(2,1)S(1)}, bf16[512,768]{1,0:T(8,128)(2,1)}, u32[]{:S(2)}, u32[]{:S(2)}) collective-permute-start(bf16[512,768]{1,0:T(8,128)(2,1)S(1)} %copy-done.7), channel_id=1, source_target_pairs={{0,16},{1,17},{2,18},{3,19},{4,20},{5,21},{6,22},{7,23},{8,24},{9,... | collective-permute-start | bytes 2359304 | tf_op jit(solution)/shard_map/ppermute | solution.py:15
  11.6 69.6 %all-reduce.3.cloned.1.call-start = ((), (), s32[]{:S(2)}) async-start(), calls=%async_computation.3 | async-start | bytes 7077888 | tf_op jit(solution)/shard_map/psum | solution.py:110
  24.0 12.1 %copy-start.8 = (f32[512,1]{0,1:T(1,128)S(1)}, f32[512,1]{0,1:T(1,128)}, u32[]{:S(2)}) copy-start(f32[512,1]{0,1:T(1,128)} %param.10) | copy-start | bytes 6148
  32.7 3.4 %copy-start.9 = (f32[512,768]{1,0:T(8,128)S(1)}, f32[512,768]{1,0:T(8,128)}, u32[]{:S(2)}) copy-start(f32[512,768]{1,0:T(8,128)} %fusion.21) | copy-start | bytes 4718596
  34.9 1.1 %copy-start.11 = (f32[512,768]{1,0:T(8,128)}, f32[512,768]{1,0:T(8,128)S(1)}, u32[]{:S(2)}) copy-start(f32[512,768]{1,0:T(8,128)S(1)} %fusion.16) | copy-start | bytes 4718596
  44.7 2.3 %copy-start.10 = (f32[512,768]{1,0:T(8,128)S(1)}, f32[512,768]{1,0:T(8,128)}, u32[]{:S(2)}) copy-start(f32[512,768]{1,0:T(8,128)} %fusion.21) | copy-start | bytes 4718596
  44.7 2.3 %copy-start.12 = (f32[512,768]{1,0:T(8,128)S(1)}, f32[512,768]{1,0:T(8,128)}, u32[]{:S(2)}) copy-start(f32[512,768]{1,0:T(8,128)} %copy-done.11) | copy-start | bytes 4718596
  51.3 1.1 %copy-start.1 = (bf16[512,768]{1,0:T(8,128)(2,1)S(1)}, bf16[512,768]{1,0:T(8,128)(2,1)}, u32[]{:S(2)}) copy-start(bf16[512,768]{1,0:T(8,128)(2,1)} %param.7) | copy-start | bytes 2359300
  61.5 12.6 %copy-start.2 = (bf16[1024,768]{0,1:T(8,128)(2,1)S(1)}, bf16[1024,768]{0,1:T(8,128)(2,1)}, u32[]{:S(2)}) copy-start(bf16[1024,768]{0,1:T(8,128)(2,1)} %copy.13) | copy-start | bytes 4718596
  81.3 3.7 %copy-start.3 = (bf16[1,768,768]{2,1,0:T(8,128)(2,1)S(1)}, bf16[1,768,768]{2,1,0:T(8,128)(2,1)}, u32[]{:S(2)}) copy-start(bf16[1,768,768]{2,1,0:T(8,128)(2,1)} %all-gather.6.cloned.1.call-done) | copy-start | bytes 3538948
  81.3 3.7 %copy-start.4 = (bf16[768,768]{1,0:T(8,128)(2,1)S(1)}, bf16[768,768]{1,0:T(8,128)(2,1)}, u32[]{:S(2)}) copy-start(bf16[768,768]{1,0:T(8,128)(2,1)} %get-tuple-element.12) | copy-start | bytes 3538948
  84.9 1.3 %copy-start.5 = (bf16[1,768,768]{2,1,0:T(8,128)(2,1)S(1)}, bf16[1,768,768]{2,1,0:T(8,128)(2,1)}, u32[]{:S(2)}) copy-start(bf16[1,768,768]{2,1,0:T(8,128)(2,1)} %all-gather.4.cloned.1.call-done) | copy-start | bytes 3538948
  84.9 1.6 %copy-start.6 = (bf16[768,768]{1,0:T(8,128)(2,1)S(1)}, bf16[768,768]{1,0:T(8,128)(2,1)}, u32[]{:S(2)}) copy-start(bf16[768,768]{1,0:T(8,128)(2,1)} %get-tuple-element.13) | copy-start | bytes 3538948
Sparse Core Ops, SparseCore 0:
  9.5 11.1 all-gather.3
  22.3 10.3 all-gather.7
  34.3 10.3 all-gather.5
  51.4 25.4 all-reduce.2
where the time goes:
time: 101 us; the launch traced here: 100 us
  matrix products  39.9 us (40%)
  waiting for transfers between devices  25.4 us (25%)
  between operations  14 us (14%)
  other arithmetic  10.7 us (11%)
  local copies, waits for them, and re-layouts  7.44 us (7%)
  starting transfers between devices  2.74 us (3%)
    sub x1, matrix products, window_block(): powers = jnp.exp(scores - row_max)  12.6 us
    all_gather x1, waiting for transfers between devices, body(): lax.all_gather(w_gate, 'context', axis=1, tiled=True)  8.8 us
    all_gather x1, waiting for transfers between devices, body(): lax.all_gather(w_up, 'context', axis=1, tiled=True)  8.71 us
    all_gather x1, waiting for transfers between devices, body(): lax.all_gather(w_down, 'context', axis=1, tiled=True)  6.47 us
    dot_general x3, matrix products, dot_rows(): lax.dot_general(first_op, second_op, (((0,), (0,)), ((), ())), preferred_...  6.47 us
    dot_general x1, matrix products, window_block(): jnp.einsum('hij,jhd->ihd', weights, values_near, preferred_element_type=j...  6.04 us
    unnamed x29, local copies, waits for them, and re-layouts  5.79 us
    dot_general x1, matrix products, apply_fast(): jnp.dot(hidden_new, down_w, preferred_element_type=jnp.float32)  5.05 us
  transfers between devices with their start and end apart: 6, of which 3 were waited for; matrix products, arithmetic and copies ran while one was open for 43% of the time, Pallas kernels for 0%

commit v1 on v0

--- a/solution.py
+++ b/solution.py
@@ -1,8 +1,11 @@
+import functools
 import math
 
 import jax
 import jax.numpy as jnp
 from jax import lax
+from jax.experimental import pallas as pl
+from jax.experimental.pallas import tpu as pltpu
 from jax.sharding import PartitionSpec as P
 
 HD = 128
@@ -66,7 +69,7 @@
     return jnp.dot(hidden_new, down_w, preferred_element_type=jnp.float32).astype(jnp.bfloat16)
 
 
-def body(query_rows, key_rows, value_rows, step_sizes, w_gate, w_up, w_down):
+def ring_body(query_rows, key_rows, value_rows, step_sizes, w_gate, w_up, w_down):
     row_count = query_rows.shape[0]
     heads_here = query_rows.shape[1] // HD
     rim_keys, rim_values = passed_along((key_rows, value_rows), "context", 1)
@@ -116,6 +119,335 @@
     return (window_out, fast_out)
 
 
+TILE = 256
+LOWEST = -1e30
+EXP_SCALE = math.log2(math.e) / math.sqrt(HD)
+ON_CHIP = pl.BlockSpec(memory_space=pltpu.VMEM)
+FAR_OFF = pl.BlockSpec(memory_space=pltpu.HBM)
+
+
+def call(kernel, outs, operands, scratch=(), flops=0, transcendentals=0, loaded=(), stored=()):
+    moved = sum(x.size * x.dtype.itemsize for x in operands)
+    moved += sum(math.prod(x.shape) * x.dtype.itemsize for x in outs)
+    operands = [
+        pltpu.with_memory_space_constraint(x, pltpu.HBM) if i in loaded else x
+        for i, x in enumerate(operands)
+    ]
+    return pl.pallas_call(
+        kernel,
+        out_shape=outs,
+        in_specs=[FAR_OFF if i in loaded else ON_CHIP for i in range(len(operands))],
+        out_specs=[FAR_OFF if i in stored else ON_CHIP for i in range(len(outs))],
+        scratch_shapes=scratch,
+        compiler_params=pltpu.CompilerParams(vmem_limit_bytes=40 * 2**20),
+        cost_estimate=pl.CostEstimate(
+            flops=flops, bytes_accessed=moved, transcendentals=transcendentals
+        ),
+    )(*operands)
+
+
+def staggered(units, begin, end, depth=1):
+    open_units = []
+    for unit in units:
+        open_units.append((unit, begin(unit)))
+        if len(open_units) > depth:
+            end(*open_units.pop(0))
+    for entry in open_units:
+        end(*entry)
+
+
+def swapped(x):
+    return lax.ppermute(x, "context", [(0, 1), (1, 0)])
+
+
+def dot_f32(first_op, second_op):
+    return jnp.dot(first_op, second_op, preferred_element_type=jnp.float32)
+
+
+def row_scale(rows):
+    wide = rows.astype(jnp.float32)
+    return lax.rsqrt(jnp.mean(wide * wide, axis=-1, keepdims=True) + 1e-06)
+
+
+def head_cols(head):
+    return slice(head * HD, (head + 1) * HD)
+
+
+def row_tiles(rows):
+    return [slice(first, first + TILE) for first in range(0, rows, TILE)]
+
+
+def key_query_order(rows):
+    key_pos = lax.broadcasted_iota(jnp.int32, (rows, rows), 0)
+    query_pos = lax.broadcasted_iota(jnp.int32, (rows, rows), 1)
+    return key_pos, query_pos
+
+
+def half_of(index, half):
+    return pl.ds(pl.multiple_of(index * half, HD), half)
+
+
+def local_kernel(
+    q_hbm, k_hbm, v_hbm, gate_hbm, up_hbm, down_hbm,
+    q_ref, k_ref, v_ref, gate_ref, up_ref, down_ref, o_ref, stats_ref, sems,
+):
+    rows, width = q_ref.shape
+    half = down_ref.shape[0]
+    mine = half_of(lax.axis_index("context"), half)
+    copies = [
+        pltpu.make_async_copy(source, target, sems.at[number])
+        for number, (source, target) in enumerate(
+            (
+                (q_hbm, q_ref),
+                (k_hbm, k_ref),
+                (v_hbm, v_ref),
+                (gate_hbm.at[:, mine], gate_ref),
+                (up_hbm.at[:, mine], up_ref),
+                (down_hbm, down_ref),
+            )
+        )
+    ]
+    for copy in copies:
+        copy.start()
+    for copy in copies[:3]:
+        copy.wait()
+    key_pos, query_pos = key_query_order(rows)
+    allowed = key_pos <= query_pos
+
+    def begin(head):
+        return dot_back(k_ref[:, head_cols(head)], q_ref[:, head_cols(head)])
+
+    def end(head, scores):
+        cols = head_cols(head)
+        scores = jnp.where(allowed, scores, LOWEST)
+        top = jnp.max(scores, axis=0, keepdims=True)
+        powers = jnp.exp2((scores - top) * EXP_SCALE)
+        stats_ref[head : head + 1, :] = top
+        stats_ref[8 + head : 9 + head, :] = jnp.sum(powers, axis=0, keepdims=True)
+        o_ref[cols, :] = dot_rows(v_ref[:, cols], powers.astype(jnp.bfloat16))
+
+    staggered(range(width // HD), begin, end)
+    for copy in copies[3:]:
+        copy.wait()
+
+
+def slopes(keys, values, steps, gate_w, up_w, down_w, d_gate, d_up, stepped):
+    half = down_w.shape[0]
+    across = jnp.transpose(jnp.broadcast_to(-steps[...], (HD, steps.shape[1])))
+
+    def begin(here):
+        return (
+            dot_f32(keys[here, :], gate_w[...]),
+            dot_f32(keys[here, :], up_w[...]),
+            dot_back(values[here, :], down_w[...]),
+        )
+
+    def end(here, products):
+        scale = jnp.broadcast_to(row_scale(keys[here, :]), (TILE, HD))
+        rate = across[here, :]
+        scale, rate, both = (
+            jnp.concatenate([x] * (half // HD), axis=1) for x in (scale, rate, rate * scale)
+        )
+        gate_pre = products[0] * scale
+        up_pre = products[1] * scale
+        back = products[2] * both
+        sigmoid_gate = jax.nn.sigmoid(gate_pre)
+        silu = gate_pre * sigmoid_gate
+        stepped[here, :] = (silu * up_pre * rate).astype(jnp.bfloat16)
+        d_up[here, :] = (back * silu).astype(jnp.bfloat16)
+        d_gate[here, :] = (
+            back * up_pre * (sigmoid_gate + silu * (1.0 - sigmoid_gate))
+        ).astype(jnp.bfloat16)
+
+    staggered(row_tiles(keys.shape[0]), begin, end)
+
+
+def near_kernel(
+    k_ref, v_ref, step_ref, gate_ref, up_ref, down_ref, gate_far_ref, up_far_ref,
+    gate_w, up_w, d_gate, d_up, stepped,
+):
+    half = down_ref.shape[0]
+    me = lax.axis_index("context")
+    mine, far = half_of(me, half), half_of(1 - me, half)
+    gate_w[mine, :] = gate_ref[...]
+    gate_w[far, :] = gate_far_ref[:, mine]
+    up_w[mine, :] = up_ref[...]
+    up_w[far, :] = up_far_ref[:, mine]
+    slopes(k_ref, v_ref, step_ref, gate_w, up_w, down_ref, d_gate, d_up, stepped)
+
+
+def far_kernel(
+    k_ref, v_ref, d_gate, d_up, stepped, k_far_ref, v_far_ref, step_far_ref,
+    gate_w, up_w, down_w, pack_ref, sums_ref, d_gate_far, d_up_far, stepped_far,
+):
+    half, width = down_w.shape
+    slopes(
+        k_far_ref, v_far_ref, step_far_ref, gate_w, up_w, down_w, d_gate_far, d_up_far, stepped_far
+    )
+    for weight, near, far, place in (
+        (gate_w, d_gate, d_gate_far, 0),
+        (up_w, d_up, d_up_far, half),
+    ):
+        initial = weight[...].astype(jnp.float32)
+        old_ms = jnp.mean(initial * initial, axis=0, keepdims=True)
+        fresh = initial - (dot_rows(k_ref[...], near[...]) + dot_rows(k_far_ref[...], far[...]))
+        new_ms = jnp.mean(fresh * fresh, axis=0, keepdims=True)
+        updated = fresh * (jnp.sqrt(old_ms) * lax.rsqrt(new_ms + 1e-06))
+        pack_ref[:width, place : place + half] = updated.astype(jnp.bfloat16)
+    initial = down_w[...].astype(jnp.float32)
+    sums_ref[0:1, :] = jnp.sum(initial * initial, axis=0, keepdims=True)
+    fresh = initial - (
+        dot_rows(stepped[...], v_ref[...]) + dot_rows(stepped_far[...], v_far_ref[...])
+    )
+    pack_ref[width:, :] = fresh.astype(jnp.bfloat16)
+    sums_ref[1:2, :] = jnp.sum(fresh * fresh, axis=0, keepdims=True)
+
+
+def half_applied(q_ref, pack_ref, store):
+    rows, width = q_ref.shape
+    half = pack_ref.shape[0] - width
+
+    def begin(here):
+        return dot_f32(q_ref[here, :], pack_ref[:width, :])
+
+    def end(here, pre):
+        pre = pre * row_scale(q_ref[here, :])
+        gate_new, up_new = pre[:, :half], pre[:, half:]
+        hidden = (gate_new * jax.nn.sigmoid(gate_new) * up_new).astype(jnp.bfloat16)
+        store(here, dot_f32(hidden, pack_ref[width:, :]))
+
+    staggered(row_tiles(rows), begin, end)
+
+
+def prior_kernel(q_ref, k_ref, v_ref, o_ref, stats_ref, pack_ref, out_hbm, part_ref, out_ref, sems):
+    rows, width = q_ref.shape
+    heads = width // HD
+
+    def store(here, part):
+        part_ref[here, :] = part
+
+    half_applied(q_ref, pack_ref, store)
+    key_pos, query_pos = key_query_order(rows)
+    allowed = key_pos > query_pos + jnp.where(lax.axis_index("context") > 0, 0, rows)
+
+    def written(head):
+        cols = head_cols(head)
+        return pltpu.make_async_copy(out_ref.at[:, cols], out_hbm.at[:, cols], sems.at[head])
+
+    def begin(head):
+        return dot_back(k_ref[:, head_cols(head)], q_ref[:, head_cols(head)])
+
+    def end(head, scores):
+        cols = head_cols(head)
+        past_top = stats_ref[head : head + 1, :]
+        scores = jnp.where(allowed, scores, LOWEST)
+        top = jnp.maximum(past_top, jnp.max(scores, axis=0, keepdims=True))
+        shrink = jnp.exp2((past_top - top) * EXP_SCALE)
+        powers = jnp.exp2((scores - top) * EXP_SCALE)
+        total = stats_ref[8 + head : 9 + head, :] * shrink
+        total += jnp.sum(powers, axis=0, keepdims=True)
+        out = o_ref[cols, :] * shrink + dot_rows(v_ref[:, cols], powers.astype(jnp.bfloat16))
+        out_ref[:, cols] = jnp.transpose(out * (1.0 / total)).astype(jnp.bfloat16)
+        written(head).start()
+
+    staggered(range(heads), begin, end)
+    for head in range(heads):
+        written(head).wait()
+
+
+def finish_kernel(q_ref, pack_ref, part_ref, sums_ref, sums_far_ref, out_hbm, out_ref, sems):
+    rows, width = q_ref.shape
+    sums = (sums_ref[0:2, :] + sums_far_ref[0:2, :]) / width
+    scale = jnp.sqrt(sums[0:1, :]) * lax.rsqrt(sums[1:2, :] + 1e-06)
+    tiles = row_tiles(rows)
+
+    def written(here):
+        return pltpu.make_async_copy(
+            out_ref.at[here, :], out_hbm.at[here, :], sems.at[tiles.index(here)]
+        )
+
+    def store(here, part):
+        out_ref[here, :] = ((part_ref[here, :] + part) * scale).astype(jnp.bfloat16)
+        written(here).start()
+
+    half_applied(q_ref, pack_ref, store)
+    for here in tiles:
+        written(here).wait()
+
+
+def shape_of(*shape, dtype=jnp.float32):
+    return jax.ShapeDtypeStruct(shape, dtype)
+
+
+def pair_body(query_rows, key_rows, value_rows, step_sizes, w_gate, w_up, w_down):
+    rows, width = query_rows.shape
+    half = w_down.shape[1]
+    w_gate, w_up, w_down = w_gate[0], w_up[0], w_down[0]
+    steps = step_sizes.reshape(1, rows)
+    gate_far, up_far = swapped(w_gate), swapped(w_up)
+    keys_far, values_far = swapped(key_rows), swapped(value_rows)
+    steps_far = swapped(steps)
+    brief = functools.partial(shape_of, dtype=jnp.bfloat16)
+    scores = rows * rows * width
+    matmul = 2 * rows * width * half
+    queries, keys, values, gate, up, down, own_out, stats = call(
+        local_kernel,
+        (
+            *(brief(rows, width),) * 3, *(brief(half, half),) * 2, brief(half, width),
+            shape_of(width, rows), shape_of(16, rows),
+        ),
+        (query_rows, key_rows, value_rows, w_gate, w_up, w_down),
+        scratch=[pltpu.SemaphoreType.DMA((6,))],
+        flops=4 * scores,
+        transcendentals=scores // HD,
+        loaded=range(6),
+    )
+    gate_w, up_w, d_gate, d_up, stepped = call(
+        near_kernel,
+        (*(brief(width, half),) * 2, *(brief(rows, half),) * 3),
+        (keys, values, steps, gate, up, down, gate_far, up_far),
+        flops=3 * matmul,
+        transcendentals=rows * half,
+    )
+    pack, sums = call(
+        far_kernel,
+        (brief(width + half, width), shape_of(8, width)),
+        (
+            keys, values, d_gate, d_up, stepped, keys_far, values_far, steps_far,
+            gate_w, up_w, down,
+        ),
+        scratch=[pltpu.VMEM((rows, half), jnp.bfloat16)] * 3,
+        flops=9 * matmul,
+        transcendentals=rows * half,
+    )
+    pack_far, sums_far = swapped(pack), swapped(sums)
+    window_out, part = call(
+        prior_kernel,
+        (brief(rows, width), shape_of(rows, width)),
+        (queries, keys_far, values_far, own_out, stats, pack),
+        scratch=[pltpu.VMEM((rows, width), jnp.bfloat16), pltpu.SemaphoreType.DMA((width // HD,))],
+        flops=4 * scores + 3 * matmul,
+        transcendentals=scores // HD + rows * half,
+        stored=(0,),
+    )
+    (fast_out,) = call(
+        finish_kernel,
+        (brief(rows, width),),
+        (queries, pack_far, part, sums, sums_far),
+        scratch=[pltpu.VMEM((rows, width), jnp.bfloat16), pltpu.SemaphoreType.DMA((rows // TILE,))],
+        flops=3 * matmul,
+        transcendentals=rows * half,
+        stored=(0,),
+    )
+    return (window_out, fast_out)
+
+
+def body(*arrays):
+    rows = arrays[0].shape[0]
+    pair = lax.axis_size("context") == 2 and rows == WINDOW and rows % TILE == 0
+    return (pair_body if pair else ring_body)(*arrays)
+
+
 def solution(mesh):
     in_specs = (
         P(("seqs", "context"), "fheads"),

time: 101 us -> 20 us (0.20)
  matrix products: 39.9 us -> 0 us
  waiting for transfers between devices: 25.4 us -> 0.51 us
  Pallas kernels: 0 us -> 16.3 us
  between operations: 14 us -> 0.71 us
  other arithmetic: 10.7 us -> 0 us
  local copies, waits for them, and re-layouts: 7.44 us -> 0.01 us
    dot_general x9 -> x0, matrix products: 27.4 us -> none  [the longest x3 6.47 us: dot_rows(): lax.dot_general(first_op, second_op, (((0,), (0,)), ((), ())), preferred_...]
    all_gather x3 -> x0, waiting for transfers between devices: 24 us -> none  [the longest x1 8.8 us: body(): lax.all_gather(w_gate, 'context', axis=1, tiled=True)]
    pallas_call x0 -> x5, Pallas kernels: none -> 16.3 us  [call(): pl.pallas_call(kernel, out_shape=outs, in_specs=[FAR_OFF if i in loaded e...]
    sub x1 -> x0, matrix products: 12.6 us -> none  [window_block(): powers = jnp.exp(scores - row_max)]
    unnamed x29 -> x2, local copies, waits for them, and re-layouts: 5.79 us -> 0.01 us
    reduce_sum x4 -> x0, other arithmetic: 4.6 us -> none  [the longest x2 4.14 us: renormed(): old_ms = jnp.mean(initial * initial, axis=0)]
    concatenate x2 -> x0, other arithmetic: 4.23 us -> none  [the longest x1 2.75 us: body(): jnp.concatenate([rim_keys, key_rows], axis=0)]
    and x1 -> x0, other arithmetic: 1.78 us -> none  [window_block(): (key_pos[None, :] >= 0) & (key_pos[None, :] <= query_pos[:, None])]
  transfers between devices with their start and end apart: 6 -> 7, of which waited for: 3 -> 1; matrix products, arithmetic and copies ran while one was open for 43% -> 0% of each run, Pallas kernels for 0% -> 51%
where the time goes in v1:
time: 20 us; the launch traced here: 19.8 us
  Pallas kernels  16.3 us (82%)
  starting transfers between devices  2.34 us (12%)
  between operations  0.71 us (4%)
  waiting for transfers between devices  0.51 us (3%)
    pallas_call x5, Pallas kernels, call(): pl.pallas_call(kernel, out_shape=outs, in_specs=[FAR_OFF if i in loaded e...  16.3 us
    ppermute x7, starting transfers between devices, swapped(): return lax.ppermute(x, 'context', [(0, 1), (1, 0)])  2.34 us
    ppermute x7, waiting for transfers between devices, swapped(): return lax.ppermute(x, 'context', [(0, 1), (1, 0)])  0.51 us
  transfers between devices with their start and end apart: 7, of which 1 were waited for; matrix products, arithmetic and copies ran while one was open for 0% of the time, Pallas kernels for 51%

profile of v1, /device:TPU:3, one launch (start us, length us, event | category | flops | bytes accessed | tf_op | source)
XLA Modules:
  0.0 19.8 jit_solution(17192647218089845662)
XLA Ops:
  0.6 0.7 %collective-permute-start = (bf16[512,768]{1,0:T(8,128)(2,1)}, bf16[512,768]{1,0:T(8,128)(2,1)S(1)}, u32[]{:S(2)}, u32[]{:S(2)}) collective-permute-start(bf16[512,768]{1,0:T(8,128)(2,1)} %k_hbm.1), channel_id=1, source_target_pairs={{0,16},{16,0},{1,17},{17,1},{2,18},{18,2},{3,19},{19,3},{4,20},{20... | collective-permute-start | bytes 2359304 | tf_op jit(solution)/shard_map/ppermute | solution.py:160
  1.4 0.1 collective-permute-start.1
  1.5 0.4 %collective-permute-start.2 = (bf16[384,768]{1,0:T(8,128)(2,1)}, bf16[384,768]{1,0:T(8,128)(2,1)S(1)}, u32[]{:S(2)}, u32[]{:S(2)}) collective-permute-start(bf16[384,768]{1,0:T(8,128)(2,1)} %bitcast.7), channel_id=1, source_target_pairs={{0,16},{16,0},{1,17},{17,1},{2,18},{18,2},{3,19},{19,3},{4,20},{20... | collective-permute-start | bytes 1769480 | tf_op jit(solution)/shard_map/ppermute | solution.py:160
  1.9 0.1 collective-permute-start.3
  2.0 0.4 %collective-permute-start.4 = (f32[1,512]{1,0:T(1,128)}, f32[1,512]{1,0:T(1,128)S(1)}, u32[]{:S(2)}, u32[]{:S(2)}) collective-permute-start(f32[1,512]{1,0:T(1,128)} %bitcast.4), channel_id=1, source_target_pairs={{0,16},{16,0},{1,17},{17,1},{2,18},{18,2},{3,19},{19,3},{4,20},{20... | collective-permute-start | bytes 6152 | tf_op jit(solution)/shard_map/ppermute | solution.py:160
  2.4 0.0 copy-start
  2.4 3.4 %shard_map.86 = (bf16[512,768]{1,0:T(8,128)(2,1)S(1)}, bf16[512,768]{1,0:T(8,128)(2,1)S(1)}, bf16[512,768]{1,0:T(8,128)(2,1)S(1)}, bf16[384,384]{1,0:T(8,128)(2,...) custom-call(bf16[512,768]{1,0:T(8,128)(2,1)} %q_hbm.1, ...), custom_call_target="tpu_custom_call" | custom-call | flops 805306368 | bytes 9273344 | tf_op jit(solution)/shard_map/pallas_call | solution.py:136
  5.8 0.0 collective-permute-done.2.gate_far_ref
  5.8 0.5 %collective-permute-done.3.up_far_ref = bf16[384,768]{1,0:T(8,128)(2,1)S(1)} collective-permute-done((bf16[384,768]{1,0:T(8,128)(2,1)}, bf16[384,768]{1,0:T(8,128)(2,1)S(1)}, u32[]{:S(2)}, u32[]{:S(2)}) %collective-permute-start.3) | collective-permute-done | bytes 589856 | tf_op jit(solution)/shard_map/ppermute | solution.py:160
  6.3 0.0 copy-done
  6.3 1.7 %shard_map.87 = (bf16[768,384]{1,0:T(8,128)(2,1)S(1)}, bf16[768,384]{1,0:T(8,128)(2,1)S(1)}, bf16[512,384]{1,0:T(8,128)(2,1)S(1)}, bf16[512,384]{1,0:T(8,128)(2,1)S(1)}, bf16[512,384]{1,0:T(8,128)(2,1)S(1)}) custom-call(bf16[512,768]{1,0:T(8,128)(2,1)S(1)} %get-tuple-element.22.k_ref, bf16[512,768]{1,0:T(8,128)(2,1)S(1)} %get-tuple-element.23.v_ref, ...), custom_call_target="tpu_custom_call" | custom-call | flops 905969664 | bytes 6293504 | tf_op jit(solution)/shard_map/pallas_call | solution.py:136
  8.0 0.0 collective-permute-done.4.step_far_ref
  8.0 0.0 collective-permute-done.k_far_ref.k_ref
  8.0 0.0 collective-permute-done.1.v_far_ref.v_ref
  8.0 4.2 %shard_map.88 = (bf16[1152,768]{1,0:T(8,128)(2,1)S(1)}, f32[8,768]{1,0:T(8,128)S(1)}) custom-call(bf16[512,768]{1,0:T(8,128)(2,1)S(1)} %get-tuple-element.22.k_ref, bf16[512,768]{1,0:T(8,128)(2,1)S(1)} %get-tuple-element.23.v_ref, bf16[512,384]{1,0:T(8,128)(2,1)S(1)} %get-tuple-element.27.d_gate, bf16[512,384]{1,0:T(8,128)(2,1)S(1)} %get-tuple-element.28.d_up, ...), custom_call_target="tpu_custom_call" | custom-call | flops 2717908992 | bytes 7890944 | tf_op jit(solution)/shard_map/pallas_call | solution.py:136
  12.2 0.4 %collective-permute-start.5 = (bf16[1152,768]{1,0:T(8,128)(2,1)S(1)}, bf16[1152,768]{1,0:T(8,128)(2,1)S(1)}, u32[]{:S(2)}, u32[]{:S(2)}) collective-permute-start(bf16[1152,768]{1,0:T(8,128)(2,1)S(1)} %get-tuple-element.32.pack_ref), channel_id=1, source_target_pairs={{0,16},{16,0},{1,17},{17,1},{2,18},{18,2},{3,19},{19,3},{4,20},{20... | collective-permute-start | bytes 5308424 | tf_op jit(solution)/shard_map/ppermute | solution.py:160
  12.7 0.1 collective-permute-start.6
  12.8 5.0 %shard_map.89 = (bf16[512,768]{1,0:T(8,128)(2,1)}, f32[512,768]{1,0:T(8,128)S(1)}) custom-call(bf16[512,768]{1,0:T(8,128)(2,1)S(1)} %get-tuple-element.19.q_ref, bf16[512,768]{1,0:T(8,128)(2,1)S(1)} %collective-permute-done.k_far_ref.k_ref, bf16[512,768]{1,0:T(8,128)(2,1)S(1)} %collective-permute-done.1.v_far_ref.v_ref, ...), custom_call_target="tpu_custom_call" | custom-call | flops 1711276032 | bytes 8093696 | tf_op jit(solution)/shard_map/pallas_call | solution.py:136
  17.8 0.0 collective-permute-done.6.sums_far_ref
  17.8 0.0 collective-permute-done.5.pack_ref
  17.9 2.0 %shard_map.90 = bf16[512,768]{1,0:T(8,128)(2,1)} custom-call(bf16[512,768]{1,0:T(8,128)(2,1)S(1)} %get-tuple-element.19.q_ref, bf16[1152,768]{1,0:T(8,128)(2,1)S(1)} %collective-permute-done.5.pack_ref, f32[512,768]{1,0:T(8,128)S(1)} %get-tuple-element.34.part_ref, f32[8,768]{1,0:T(8,128)S(1)} %get-tuple-element.35.sums_ref, ...), custom_call_target="tpu_custom_call" | custom-call | flops 905969664 | bytes 4964352 | tf_op jit(solution)/shard_map/pallas_call | solution.py:136
Async XLA Ops:
  0.6 7.4 %collective-permute-start = (bf16[512,768]{1,0:T(8,128)(2,1)}, bf16[512,768]{1,0:T(8,128)(2,1)S(1)}, u32[]{:S(2)}, u32[]{:S(2)}) collective-permute-start(bf16[512,768]{1,0:T(8,128)(2,1)} %k_hbm.1), channel_id=1, source_target_pairs={{0,16},{16,0},{1,17},{17,1},{2,18},{18,2},{3,19},{19,3},{4,20},{20... | collective-permute-start | bytes 2359304 | tf_op jit(solution)/shard_map/ppermute | solution.py:160
  1.4 6.7 %collective-permute-start.1 = (bf16[512,768]{1,0:T(8,128)(2,1)}, bf16[512,768]{1,0:T(8,128)(2,1)S(1)}, u32[]{:S(2)}, u32[]{:S(2)}) collective-permute-start(bf16[512,768]{1,0:T(8,128)(2,1)} %v_hbm.1), channel_id=1, source_target_pairs={{0,16},{16,0},{1,17},{17,1},{2,18},{18,2},{3,19},{19,3},{4,20},{20... | collective-permute-start | bytes 2359304 | tf_op jit(solution)/shard_map/ppermute | solution.py:160
  1.5 4.3 %collective-permute-start.2 = (bf16[384,768]{1,0:T(8,128)(2,1)}, bf16[384,768]{1,0:T(8,128)(2,1)S(1)}, u32[]{:S(2)}, u32[]{:S(2)}) collective-permute-start(bf16[384,768]{1,0:T(8,128)(2,1)} %bitcast.7), channel_id=1, source_target_pairs={{0,16},{16,0},{1,17},{17,1},{2,18},{18,2},{3,19},{19,3},{4,20},{20... | collective-permute-start | bytes 1769480 | tf_op jit(solution)/shard_map/ppermute | solution.py:160
  1.9 4.4 %collective-permute-start.3 = (bf16[384,768]{1,0:T(8,128)(2,1)}, bf16[384,768]{1,0:T(8,128)(2,1)S(1)}, u32[]{:S(2)}, u32[]{:S(2)}) collective-permute-start(bf16[384,768]{1,0:T(8,128)(2,1)} %bitcast.9), channel_id=1, source_target_pairs={{0,16},{16,0},{1,17},{17,1},{2,18},{18,2},{3,19},{19,3},{4,20},{20... | collective-permute-start | bytes 1769480 | tf_op jit(solution)/shard_map/ppermute | solution.py:160
  2.0 6.1 %collective-permute-start.4 = (f32[1,512]{1,0:T(1,128)}, f32[1,512]{1,0:T(1,128)S(1)}, u32[]{:S(2)}, u32[]{:S(2)}) collective-permute-start(f32[1,512]{1,0:T(1,128)} %bitcast.4), channel_id=1, source_target_pairs={{0,16},{16,0},{1,17},{17,1},{2,18},{18,2},{3,19},{19,3},{4,20},{20... | collective-permute-start | bytes 6152 | tf_op jit(solution)/shard_map/ppermute | solution.py:160
  2.4 3.9 %copy-start = (f32[512,1]{0,1:T(1,128)S(1)}, f32[512,1]{0,1:T(1,128)}, u32[]{:S(2)}) copy-start(f32[512,1]{0,1:T(1,128)} %param.10) | copy-start | bytes 6148
  12.2 5.6 %collective-permute-start.5 = (bf16[1152,768]{1,0:T(8,128)(2,1)S(1)}, bf16[1152,768]{1,0:T(8,128)(2,1)S(1)}, u32[]{:S(2)}, u32[]{:S(2)}) collective-permute-start(bf16[1152,768]{1,0:T(8,128)(2,1)S(1)} %get-tuple-element.32.pack_ref), channel_id=1, source_target_pairs={{0,16},{16,0},{1,17},{17,1},{2,18},{18,2},{3,19},{19,3},{4,20},{20... | collective-permute-start | bytes 5308424 | tf_op jit(solution)/shard_map/ppermute | solution.py:160
  12.7 5.2 %collective-permute-start.6 = (f32[8,768]{1,0:T(8,128)S(1)}, f32[8,768]{1,0:T(8,128)S(1)}, u32[]{:S(2)}, u32[]{:S(2)}) collective-permute-start(f32[8,768]{1,0:T(8,128)S(1)} %get-tuple-element.35.sums_ref), channel_id=1, source_target_pairs={{0,16},{16,0},{1,17},{17,1},{2,18},{18,2},{3,19},{19,3},{4,20},{20... | collective-permute-start | bytes 73736 | tf_op jit(solution)/shard_map/ppermute | solution.py:160

commit v2 on v1

--- a/solution.py
+++ b/solution.py
@@ -7,6 +7,7 @@
 from jax.experimental import pallas as pl
 from jax.experimental.pallas import tpu as pltpu
 from jax.sharding import PartitionSpec as P
+
 
 HD = 128
 WINDOW = 512
@@ -177,10 +178,14 @@
     return [slice(first, first + TILE) for first in range(0, rows, TILE)]
 
 
-def key_query_order(rows):
-    key_pos = lax.broadcasted_iota(jnp.int32, (rows, rows), 0)
-    query_pos = lax.broadcasted_iota(jnp.int32, (rows, rows), 1)
+def key_query_order():
+    key_pos = lax.broadcasted_iota(jnp.int32, (TILE, TILE), 0)
+    query_pos = lax.broadcasted_iota(jnp.int32, (TILE, TILE), 1)
     return key_pos, query_pos
+
+
+def head_units(rows, width):
+    return [(head, here) for head in range(width // HD) for here in row_tiles(rows)]
 
 
 def half_of(index, half):
@@ -194,40 +199,41 @@
     rows, width = q_ref.shape
     half = down_ref.shape[0]
     mine = half_of(lax.axis_index("context"), half)
-    copies = [
-        pltpu.make_async_copy(source, target, sems.at[number])
-        for number, (source, target) in enumerate(
-            (
-                (q_hbm, q_ref),
-                (k_hbm, k_ref),
-                (v_hbm, v_ref),
-                (gate_hbm.at[:, mine], gate_ref),
-                (up_hbm.at[:, mine], up_ref),
-                (down_hbm, down_ref),
-            )
-        )
+    early, late = slice(0, 2 * HD), slice(2 * HD, width)
+    pairs = [
+        (source.at[:, cols], target.at[:, cols])
+        for cols in (early, late)
+        for source, target in ((k_hbm, k_ref), (q_hbm, q_ref), (v_hbm, v_ref))
     ]
+    pairs += [
+        (gate_hbm.at[:, mine], gate_ref), (up_hbm.at[:, mine], up_ref), (down_hbm, down_ref)
+    ]
+    copies = [pltpu.make_async_copy(*pair, sems.at[i]) for i, pair in enumerate(pairs)]
     for copy in copies:
         copy.start()
-    for copy in copies[:3]:
-        copy.wait()
-    key_pos, query_pos = key_query_order(rows)
-    allowed = key_pos <= query_pos
-
-    def begin(head):
-        return dot_back(k_ref[:, head_cols(head)], q_ref[:, head_cols(head)])
-
-    def end(head, scores):
+    key_pos, query_pos = key_query_order()
+
+    def begin(unit):
+        head, here = unit
+        if here.start == 0:
+            for copy in {0: copies[:2], 1: copies[2:3], 2: copies[3:6]}.get(head, ()):
+                copy.wait()
         cols = head_cols(head)
-        scores = jnp.where(allowed, scores, LOWEST)
+        return dot_back(k_ref[: here.stop, cols], q_ref[here, cols])
+
+    def end(unit, scores):
+        head, here = unit
+        cols = head_cols(head)
+        own = jnp.where(key_pos <= query_pos, scores[here.start :], LOWEST)
+        scores = jnp.concatenate([scores[: here.start], own]) if here.start else own
         top = jnp.max(scores, axis=0, keepdims=True)
         powers = jnp.exp2((scores - top) * EXP_SCALE)
-        stats_ref[head : head + 1, :] = top
-        stats_ref[8 + head : 9 + head, :] = jnp.sum(powers, axis=0, keepdims=True)
-        o_ref[cols, :] = dot_rows(v_ref[:, cols], powers.astype(jnp.bfloat16))
-
-    staggered(range(width // HD), begin, end)
-    for copy in copies[3:]:
+        stats_ref[head : head + 1, here] = top
+        stats_ref[8 + head : 9 + head, here] = jnp.sum(powers, axis=0, keepdims=True)
+        o_ref[cols, here] = dot_rows(v_ref[: here.stop, cols], powers.astype(jnp.bfloat16))
+
+    staggered(head_units(rows, width), begin, end, depth=2)
+    for copy in copies[6:]:
         copy.wait()
 
 
@@ -304,7 +310,7 @@
 
 
 def half_applied(q_ref, pack_ref, store):
-    rows, width = q_ref.shape
+    width = q_ref.shape[1]
     half = pack_ref.shape[0] - width
 
     def begin(here):
@@ -314,65 +320,72 @@
         pre = pre * row_scale(q_ref[here, :])
         gate_new, up_new = pre[:, :half], pre[:, half:]
         hidden = (gate_new * jax.nn.sigmoid(gate_new) * up_new).astype(jnp.bfloat16)
-        store(here, dot_f32(hidden, pack_ref[width:, :]))
-
-    staggered(row_tiles(rows), begin, end)
-
-
-def prior_kernel(q_ref, k_ref, v_ref, o_ref, stats_ref, pack_ref, out_hbm, part_ref, out_ref, sems):
+        for first in range(0, width, TILE):
+            cols = slice(first, first + TILE)
+            store(here, cols, dot_f32(hidden, pack_ref[width:, cols]))
+
+    return begin, end
+
+
+def prior_kernel(q_ref, k_ref, v_ref, o_ref, stats_ref, pack_ref, out_ref, part_ref):
     rows, width = q_ref.shape
-    heads = width // HD
-
-    def store(here, part):
-        part_ref[here, :] = part
-
-    half_applied(q_ref, pack_ref, store)
-    key_pos, query_pos = key_query_order(rows)
-    allowed = key_pos > query_pos + jnp.where(lax.axis_index("context") > 0, 0, rows)
-
-    def written(head):
+
+    def store(here, cols, part):
+        part_ref[here, cols] = part
+
+    begin_tile, end_tile = half_applied(q_ref, pack_ref, store)
+    key_pos, query_pos = key_query_order()
+    absent = jnp.where(lax.axis_index("context") > 0, 0.0, -LOWEST)
+
+    def begin(unit):
+        if isinstance(unit, slice):
+            return begin_tile(unit)
+        head, here = unit
         cols = head_cols(head)
-        return pltpu.make_async_copy(out_ref.at[:, cols], out_hbm.at[:, cols], sems.at[head])
-
-    def begin(head):
-        return dot_back(k_ref[:, head_cols(head)], q_ref[:, head_cols(head)])
-
-    def end(head, scores):
+        return dot_back(k_ref[here.start :, cols], q_ref[here, cols])
+
+    def end(unit, scores):
+        if isinstance(unit, slice):
+            return end_tile(unit, scores)
+        head, here = unit
         cols = head_cols(head)
-        past_top = stats_ref[head : head + 1, :]
-        scores = jnp.where(allowed, scores, LOWEST)
-        top = jnp.maximum(past_top, jnp.max(scores, axis=0, keepdims=True))
+        past_top = stats_ref[head : head + 1, here]
+        own = jnp.where(key_pos > query_pos, scores[:TILE], LOWEST)
+        scores = jnp.concatenate([own, scores[TILE:]]) if here.stop < rows else own
+        top = jnp.maximum(past_top, jnp.max(scores, axis=0, keepdims=True) - absent)
         shrink = jnp.exp2((past_top - top) * EXP_SCALE)
-        powers = jnp.exp2((scores - top) * EXP_SCALE)
-        total = stats_ref[8 + head : 9 + head, :] * shrink
+        powers = jnp.exp2((scores - (top + absent)) * EXP_SCALE)
+        total = stats_ref[8 + head : 9 + head, here] * shrink
         total += jnp.sum(powers, axis=0, keepdims=True)
-        out = o_ref[cols, :] * shrink + dot_rows(v_ref[:, cols], powers.astype(jnp.bfloat16))
-        out_ref[:, cols] = jnp.transpose(out * (1.0 / total)).astype(jnp.bfloat16)
-        written(head).start()
-
-    staggered(range(heads), begin, end)
-    for head in range(heads):
-        written(head).wait()
-
-
-def finish_kernel(q_ref, pack_ref, part_ref, sums_ref, sums_far_ref, out_hbm, out_ref, sems):
+        out = dot_rows(v_ref[here.start :, cols], powers.astype(jnp.bfloat16))
+        out = (o_ref[cols, here] * shrink + out) * (1.0 / total)
+        out_ref[here, cols] = jnp.transpose(out).astype(jnp.bfloat16)
+
+    staggered([*row_tiles(rows), *head_units(rows, width)], begin, end, depth=2)
+
+
+def finish_kernel(
+    q_ref, pack_ref, part_ref, sums_ref, sums_far_ref, window_ref, out_hbm, window_hbm, out_ref, sems
+):
     rows, width = q_ref.shape
+    window_copy = pltpu.make_async_copy(window_ref, window_hbm, sems.at[0])
+    window_copy.start()
     sums = (sums_ref[0:2, :] + sums_far_ref[0:2, :]) / width
     scale = jnp.sqrt(sums[0:1, :]) * lax.rsqrt(sums[1:2, :] + 1e-06)
     tiles = row_tiles(rows)
-
-    def written(here):
-        return pltpu.make_async_copy(
-            out_ref.at[here, :], out_hbm.at[here, :], sems.at[tiles.index(here)]
+    written = [window_copy]
+
+    def store(here, cols, part):
+        out_ref[here, cols] = ((part_ref[here, cols] + part) * scale[:, cols]).astype(jnp.bfloat16)
+        copy = pltpu.make_async_copy(
+            out_ref.at[here, cols], out_hbm.at[here, cols], sems.at[len(written)]
         )
-
-    def store(here, part):
-        out_ref[here, :] = ((part_ref[here, :] + part) * scale).astype(jnp.bfloat16)
-        written(here).start()
-
-    half_applied(q_ref, pack_ref, store)
-    for here in tiles:
-        written(here).wait()
+        copy.start()
+        written.append(copy)
+
+    staggered(tiles, *half_applied(q_ref, pack_ref, store))
+    for copy in written:
+        copy.wait()
 
 
 def shape_of(*shape, dtype=jnp.float32):
@@ -397,7 +410,7 @@
             shape_of(width, rows), shape_of(16, rows),
         ),
         (query_rows, key_rows, value_rows, w_gate, w_up, w_down),
-        scratch=[pltpu.SemaphoreType.DMA((6,))],
+        scratch=[pltpu.SemaphoreType.DMA((9,))],
         flops=4 * scores,
         transcendentals=scores // HD,
         loaded=range(6),
@@ -421,23 +434,24 @@
         transcendentals=rows * half,
     )
     pack_far, sums_far = swapped(pack), swapped(sums)
-    window_out, part = call(
+    window, part = call(
         prior_kernel,
         (brief(rows, width), shape_of(rows, width)),
         (queries, keys_far, values_far, own_out, stats, pack),
-        scratch=[pltpu.VMEM((rows, width), jnp.bfloat16), pltpu.SemaphoreType.DMA((width // HD,))],
         flops=4 * scores + 3 * matmul,
         transcendentals=scores // HD + rows * half,
-        stored=(0,),
-    )
-    (fast_out,) = call(
+    )
+    fast_out, window_out = call(
         finish_kernel,
-        (brief(rows, width),),
-        (queries, pack_far, part, sums, sums_far),
-        scratch=[pltpu.VMEM((rows, width), jnp.bfloat16), pltpu.SemaphoreType.DMA((rows // TILE,))],
+        (brief(rows, width),) * 2,
+        (queries, pack_far, part, sums, sums_far, window),
+        scratch=[
+            pltpu.VMEM((rows, width), jnp.bfloat16),
+            pltpu.SemaphoreType.DMA((1 + rows * width // TILE**2,)),
+        ],
         flops=3 * matmul,
         transcendentals=rows * half,
-        stored=(0,),
+        stored=(0, 1),
     )
     return (window_out, fast_out)
 

time: 20 us -> 18.2 us (0.910)
  Pallas kernels: 16.3 us -> 14.3 us
  waiting for transfers between devices: 0.51 us -> 0.76 us
    pallas_call x5, Pallas kernels: 16.3 us -> 14.3 us  [call(): pl.pallas_call(kernel, out_shape=outs, in_specs=[FAR_OFF if i in loaded e...]
    ppermute x7, waiting for transfers between devices: 0.51 us -> 0.76 us  [swapped(): return lax.ppermute(x, 'context', [(0, 1), (1, 0)])]
  transfers between devices with their start and end apart: 7 -> 7, of which waited for: 1 -> 1; matrix products, arithmetic and copies ran while one was open for 0% -> 0% of each run, Pallas kernels for 51% -> 44%
where the time goes in v2:
time: 18.2 us; the launch traced here: 18.1 us
  Pallas kernels  14.3 us (79%)
  starting transfers between devices  2.34 us (13%)
  waiting for transfers between devices  0.76 us (4%)
  between operations  0.7 us (4%)
    pallas_call x5, Pallas kernels, call(): pl.pallas_call(kernel, out_shape=outs, in_specs=[FAR_OFF if i in loaded e...  14.3 us
    ppermute x7, starting transfers between devices, swapped(): return lax.ppermute(x, 'context', [(0, 1), (1, 0)])  2.34 us
    ppermute x7, waiting for transfers between devices, swapped(): return lax.ppermute(x, 'context', [(0, 1), (1, 0)])  0.76 us
  transfers between devices with their start and end apart: 7, of which 1 were waited for; matrix products, arithmetic and copies ran while one was open for 0% of the time, Pallas kernels for 44%

profile of v2, /device:TPU:3, one launch (start us, length us, event | category | flops | bytes accessed | tf_op | source)
XLA Modules:
  0.0 18.1 jit_solution(12050732555789819177)
XLA Ops:
  0.6 0.7 %collective-permute-start.2 = (bf16[512,768]{1,0:T(8,128)(2,1)}, bf16[512,768]{1,0:T(8,128)(2,1)S(1)}, u32[]{:S(2)}, u32[]{:S(2)}) collective-permute-start(bf16[512,768]{1,0:T(8,128)(2,1)} %k_hbm.1), channel_id=1, source_target_pairs={{0,16},{16,0},{1,17},{17,1},{2,18},{18,2},{3,19},{19,3},{4,20},{20... | collective-permute-start | bytes 2359304 | tf_op jit(solution)/shard_map/ppermute | solution.py:161
  1.4 0.1 collective-permute-start.3
  1.5 0.4 %collective-permute-start = (bf16[384,768]{1,0:T(8,128)(2,1)}, bf16[384,768]{1,0:T(8,128)(2,1)S(1)}, u32[]{:S(2)}, u32[]{:S(2)}) collective-permute-start(bf16[384,768]{1,0:T(8,128)(2,1)} %bitcast.7), channel_id=1, source_target_pairs={{0,16},{16,0},{1,17},{17,1},{2,18},{18,2},{3,19},{19,3},{4,20},{20... | collective-permute-start | bytes 1769480 | tf_op jit(solution)/shard_map/ppermute | solution.py:161
  1.9 0.1 collective-permute-start.1
  2.0 0.4 %collective-permute-start.4 = (f32[1,512]{1,0:T(1,128)}, f32[1,512]{1,0:T(1,128)S(1)}, u32[]{:S(2)}, u32[]{:S(2)}) collective-permute-start(f32[1,512]{1,0:T(1,128)} %bitcast.4), channel_id=1, source_target_pairs={{0,16},{16,0},{1,17},{17,1},{2,18},{18,2},{3,19},{19,3},{4,20},{20... | collective-permute-start | bytes 6152 | tf_op jit(solution)/shard_map/ppermute | solution.py:161
  2.4 0.0 copy-start
  2.4 3.2 %shard_map.86 = (bf16[512,768]{1,0:T(8,128)(2,1)S(1)}, bf16[512,768]{1,0:T(8,128)(2,1)S(1)}, bf16[512,768]{1,0:T(8,128)(2,1)S(1)}, bf16[384,384]{1,0:T(8,128)(2,...) custom-call(bf16[512,768]{1,0:T(8,128)(2,1)} %q_hbm.1, ...), custom_call_target="tpu_custom_call" | custom-call | flops 805306368 | bytes 9273344 | tf_op jit(solution)/shard_map/pallas_call | solution.py:137
  5.6 0.0 collective-permute-done.gate_far_ref
  5.6 0.7 %collective-permute-done.1.up_far_ref = bf16[384,768]{1,0:T(8,128)(2,1)S(1)} collective-permute-done((bf16[384,768]{1,0:T(8,128)(2,1)}, bf16[384,768]{1,0:T(8,128)(2,1)S(1)}, u32[]{:S(2)}, u32[]{:S(2)}) %collective-permute-start.1) | collective-permute-done | bytes 589856 | tf_op jit(solution)/shard_map/ppermute | solution.py:161
  6.3 0.0 copy-done
  6.3 1.7 %shard_map.87 = (bf16[768,384]{1,0:T(8,128)(2,1)S(1)}, bf16[768,384]{1,0:T(8,128)(2,1)S(1)}, bf16[512,384]{1,0:T(8,128)(2,1)S(1)}, bf16[512,384]{1,0:T(8,128)(2,1)S(1)}, bf16[512,384]{1,0:T(8,128)(2,1)S(1)}) custom-call(bf16[512,768]{1,0:T(8,128)(2,1)S(1)} %get-tuple-element.22.k_ref, bf16[512,768]{1,0:T(8,128)(2,1)S(1)} %get-tuple-element.23.v_ref, ...), custom_call_target="tpu_custom_call" | custom-call | flops 905969664 | bytes 6293504 | tf_op jit(solution)/shard_map/pallas_call | solution.py:137
  8.0 0.0 collective-permute-done.4.step_far_ref
  8.0 0.0 collective-permute-done.2.k_far_ref.k_ref
  8.0 0.0 collective-permute-done.3.v_far_ref.v_ref
  8.0 4.3 %shard_map.88 = (bf16[1152,768]{1,0:T(8,128)(2,1)S(1)}, f32[8,768]{1,0:T(8,128)S(1)}) custom-call(bf16[512,768]{1,0:T(8,128)(2,1)S(1)} %get-tuple-element.22.k_ref, bf16[512,768]{1,0:T(8,128)(2,1)S(1)} %get-tuple-element.23.v_ref, bf16[512,384]{1,0:T(8,128)(2,1)S(1)} %get-tuple-element.27.d_gate, bf16[512,384]{1,0:T(8,128)(2,1)S(1)} %get-tuple-element.28.d_up, ...), custom_call_target="tpu_custom_call" | custom-call | flops 2717908992 | bytes 7890944 | tf_op jit(solution)/shard_map/pallas_call | solution.py:137
  12.3 0.4 %collective-permute-start.5 = (bf16[1152,768]{1,0:T(8,128)(2,1)S(1)}, bf16[1152,768]{1,0:T(8,128)(2,1)S(1)}, u32[]{:S(2)}, u32[]{:S(2)}) collective-permute-start(bf16[1152,768]{1,0:T(8,128)(2,1)S(1)} %get-tuple-element.32.pack_ref), channel_id=1, source_target_pairs={{0,16},{16,0},{1,17},{17,1},{2,18},{18,2},{3,19},{19,3},{4,20},{20... | collective-permute-start | bytes 5308424 | tf_op jit(solution)/shard_map/ppermute | solution.py:161
  12.7 0.1 collective-permute-start.6
  12.9 3.2 %shard_map.89 = (bf16[512,768]{1,0:T(8,128)(2,1)S(1)}, f32[512,768]{1,0:T(8,128)S(1)}) custom-call(bf16[512,768]{1,0:T(8,128)(2,1)S(1)} %get-tuple-element.21.q_ref, bf16[512,768]{1,0:T(8,128)(2,1)S(1)} %collective-permute-done.2.k_far_ref.k_ref, bf16[512,768]{1,0:T(8,128)(2,1)S(1)} %collective-permute-done.3.v_far_ref.v_ref, ...), custom_call_target="tpu_custom_call" | custom-call | flops 1711276032 | bytes 8093696 | tf_op jit(solution)/shard_map/pallas_call | solution.py:137
  16.1 0.0 collective-permute-done.6.sums_far_ref
  16.1 0.0 collective-permute-done.5.pack_ref
  16.1 2.0 %shard_map.90 = (bf16[512,768]{1,0:T(8,128)(2,1)}, bf16[512,768]{1,0:T(8,128)(2,1)}) custom-call(bf16[512,768]{1,0:T(8,128)(2,1)S(1)} %get-tuple-element.21.q_ref, bf16[1152,768]{1,0:T(8,128)(2,1)S(1)} %collective-permute-done.5.pack_ref, f32[512,768]{1,0:T(8,128)S(1)} %get-tuple-element.35.part_ref, f32[8,768]{1,0:T(8,128)S(1)} %get-tuple-element.36.sums_ref, ...), custom_call_target="tpu_custom_call" | custom-call | flops 905969664 | bytes 6537216 | tf_op jit(solution)/shard_map/pallas_call | solution.py:137
Async XLA Ops:
  0.6 7.4 %collective-permute-start.2 = (bf16[512,768]{1,0:T(8,128)(2,1)}, bf16[512,768]{1,0:T(8,128)(2,1)S(1)}, u32[]{:S(2)}, u32[]{:S(2)}) collective-permute-start(bf16[512,768]{1,0:T(8,128)(2,1)} %k_hbm.1), channel_id=1, source_target_pairs={{0,16},{16,0},{1,17},{17,1},{2,18},{18,2},{3,19},{19,3},{4,20},{20... | collective-permute-start | bytes 2359304 | tf_op jit(solution)/shard_map/ppermute | solution.py:161
  1.4 6.7 %collective-permute-start.3 = (bf16[512,768]{1,0:T(8,128)(2,1)}, bf16[512,768]{1,0:T(8,128)(2,1)S(1)}, u32[]{:S(2)}, u32[]{:S(2)}) collective-permute-start(bf16[512,768]{1,0:T(8,128)(2,1)} %v_hbm.1), channel_id=1, source_target_pairs={{0,16},{16,0},{1,17},{17,1},{2,18},{18,2},{3,19},{19,3},{4,20},{20... | collective-permute-start | bytes 2359304 | tf_op jit(solution)/shard_map/ppermute | solution.py:161
  1.5 4.1 %collective-permute-start = (bf16[384,768]{1,0:T(8,128)(2,1)}, bf16[384,768]{1,0:T(8,128)(2,1)S(1)}, u32[]{:S(2)}, u32[]{:S(2)}) collective-permute-start(bf16[384,768]{1,0:T(8,128)(2,1)} %bitcast.7), channel_id=1, source_target_pairs={{0,16},{16,0},{1,17},{17,1},{2,18},{18,2},{3,19},{19,3},{4,20},{20... | collective-permute-start | bytes 1769480 | tf_op jit(solution)/shard_map/ppermute | solution.py:161
  1.9 4.4 %collective-permute-start.1 = (bf16[384,768]{1,0:T(8,128)(2,1)}, bf16[384,768]{1,0:T(8,128)(2,1)S(1)}, u32[]{:S(2)}, u32[]{:S(2)}) collective-permute-start(bf16[384,768]{1,0:T(8,128)(2,1)} %bitcast.9), channel_id=1, source_target_pairs={{0,16},{16,0},{1,17},{17,1},{2,18},{18,2},{3,19},{19,3},{4,20},{20... | collective-permute-start | bytes 1769480 | tf_op jit(solution)/shard_map/ppermute | solution.py:161
  2.0 6.1 %collective-permute-start.4 = (f32[1,512]{1,0:T(1,128)}, f32[1,512]{1,0:T(1,128)S(1)}, u32[]{:S(2)}, u32[]{:S(2)}) collective-permute-start(f32[1,512]{1,0:T(1,128)} %bitcast.4), channel_id=1, source_target_pairs={{0,16},{16,0},{1,17},{17,1},{2,18},{18,2},{3,19},{19,3},{4,20},{20... | collective-permute-start | bytes 6152 | tf_op jit(solution)/shard_map/ppermute | solution.py:161
  2.4 3.9 %copy-start = (f32[512,1]{0,1:T(1,128)S(1)}, f32[512,1]{0,1:T(1,128)}, u32[]{:S(2)}) copy-start(f32[512,1]{0,1:T(1,128)} %param.10) | copy-start | bytes 6148
  12.3 3.8 %collective-permute-start.5 = (bf16[1152,768]{1,0:T(8,128)(2,1)S(1)}, bf16[1152,768]{1,0:T(8,128)(2,1)S(1)}, u32[]{:S(2)}, u32[]{:S(2)}) collective-permute-start(bf16[1152,768]{1,0:T(8,128)(2,1)S(1)} %get-tuple-element.32.pack_ref), channel_id=1, source_target_pairs={{0,16},{16,0},{1,17},{17,1},{2,18},{18,2},{3,19},{19,3},{4,20},{20... | collective-permute-start | bytes 5308424 | tf_op jit(solution)/shard_map/ppermute | solution.py:161
  12.7 3.4 %collective-permute-start.6 = (f32[8,768]{1,0:T(8,128)S(1)}, f32[8,768]{1,0:T(8,128)S(1)}, u32[]{:S(2)}, u32[]{:S(2)}) collective-permute-start(f32[8,768]{1,0:T(8,128)S(1)} %get-tuple-element.36.sums_ref), channel_id=1, source_target_pairs={{0,16},{16,0},{1,17},{17,1},{2,18},{18,2},{3,19},{19,3},{4,20},{20... | collective-permute-start | bytes 73736 | tf_op jit(solution)/shard_map/ppermute | solution.py:161
